TPU v7x, 32 devices: a whole 2x2x4 slice. The times are simulated.
32 devices in a mesh: member: 1, tile: 32 (over z, y, x, core).
Axes of the slice: x: 2, y: 2, z: 4, core: 2. Of those that a mesh axis runs over, the one named last changes fastest.
Arguments:
- forcing: bfloat16 [128, 8, 10, 128], P(('member', 'tile')), may hold values from -6 to 6
- ice_state: bfloat16 [1024, 128, 128], P(('member', 'tile')), may hold values from -6 to 6
- sensitivity: bfloat16 [1024, 128, 128], P(('member', 'tile')), may hold values from -6 to 6
- owner_device: int32 [1024, 4], P('tile'), may hold values from 0 to 31, all different within a row; in each aligned block of 32 rows (0 to 31, 32 to 63, ...) at most 8 rows name the same one
- panel_slot: int32 [1024, 4], P('tile'), may hold values from 0 to 3
- row_offset: int32 [1024, 4], P('tile'), may hold values from 0 to 7
- intersection_weight: float32 [1024, 4], P('tile'), may hold values from 0.2 to 1
- col_map: float32 [128, 128], replicated, may hold values from 0 to 1
- ocean_mask: int32 [1024, 128], P('tile'), may hold values 0 or 1
- lift_weight: bfloat16 [10, 128], replicated, may hold values from -1 to 1
- conv_weight: bfloat16 [3, 3, 3, 128, 128], replicated, may hold values from -0.1875 to 0.1875
- conv_bias: float32 [3, 128], replicated, may hold values from -3 to 3
Outputs:
- imitated: bfloat16 [1024, 128, 128], P(('member', 'tile'))
- state_grad: bfloat16 [1024, 128, 128], P(('member', 'tile'))
- forcing_grad: float32 [128, 8, 10, 128], P(('member', 'tile'))
Inputs may be any that keep to these rules, and one draw needn't show every extreme that they name: `owner_device`: each ice row names 4 different owners; in the rows of one device no owner is named by more than 8 intersections, and that count is reached.
All inputs are finite; a program needn't handle non-finite values. No bound on the sum of `ocean_mask` on one device may be relied on, other than what follows from the above.
Results may differ from a plain program's by a relative error of at most 0.015.
Values may be sent and summed in bfloat16 or wider, within the bound.
A program may use at most 128 MiB of HBM per device.

v0:
```python
import functools

import jax
import jax.numpy as jnp
from jax import lax
from jax.experimental import pallas as pl
from jax.experimental.pallas import tpu as pltpu
from jax.sharding import PartitionSpec as P

F = 10
K = 4
ROWS_DEV = 32
FP = 16
HALF = 640
BLK = 16
E = 48
f32, bf16 = jnp.float32, jnp.bfloat16


def dot(a, b, ca=1, cb=0):
    return lax.dot_general(a, b, (((ca,), (cb,)), ((), ())), preferred_element_type=f32)


def iota(shape, dim):
    return lax.broadcasted_iota(jnp.int32, shape, dim)


def remote(src, dst, send, recv, target):
    return pltpu.make_async_remote_copy(
        src_ref=src, dst_ref=dst, send_sem=send, recv_sem=recv,
        device_id={"tile": target}, device_id_type=pl.DeviceIdType.MESH,
    )


def enter(n, me):
    barrier = pltpu.get_barrier_semaphore()

    def greet(step, carry):
        pl.semaphore_signal(
            barrier, inc=1, device_id={"tile": lax.rem(me + step, n)},
            device_id_type=pl.DeviceIdType.MESH,
        )
        return carry

    lax.fori_loop(1, n, greet, 0)
    pl.semaphore_wait(barrier, n - 1)


def block(ref, p):
    return ref.at[pl.ds(pl.multiple_of(p * BLK, BLK), BLK)]


def exchange(n, me, src, dst, send, recv, start, wait):
    def begin(step, carry):
        to = lax.rem(me + step, n)
        remote(block(src, to), block(dst, me), send.at[step], recv.at[step], to).start()
        return carry

    def finish(step, carry):
        to = lax.rem(me + step, n)
        source = lax.rem(me + n - step, n)
        remote(block(src, to), block(dst, source), send.at[step], recv.at[step], to).wait()
        return carry

    if start:
        lax.fori_loop(1, n, begin, 0)
        mine = pl.ds(pl.multiple_of(me * BLK, BLK), BLK)
        dst[mine, :] = src[mine, :]
    if wait:
        lax.fori_loop(1, n, finish, 0)


def gather_kernel(
    n, ice, sens, ocean, own_c, own_r, loc_c, w_c, forc,
    pre_out, oh_out, w2_out, iceh, sensh, och,
    oh_send, oh_recv, f_send, f_recv, pre, prex,
    s1, r1, s2, r2, s3, r3,
):
    me = lax.axis_index("tile")
    right, left = lax.rem(me + 1, n), lax.rem(me + n - 1, n)
    nb = n * BLK
    nk = ROWS_DEV * K
    enter(n, me)
    own = own_c[...]
    same = own == own_r[...]
    earlier = iota((nk, nk), 1) < iota((nk, nk), 0)
    rank = jnp.sum(jnp.where(same & earlier, 1.0, 0.0), axis=1, keepdims=True).astype(jnp.int32)
    col = own * BLK + rank
    lane = iota((nk, nb), 1)
    pa = jnp.where(col == lane, 1.0, 0.0)
    pb = jnp.where(col + 8 == lane, 1.0, 0.0)
    low = iota((nk, 128), 1)
    la = jnp.where(loc_c[...] == low, 1.0, 0.0)
    lb = jnp.where(loc_c[...] + ROWS_DEV == low, 1.0, 0.0)
    oh = dot(pa.astype(bf16), la.astype(bf16), 0, 0) + dot(pb.astype(bf16), lb.astype(bf16), 0, 0)
    oh_send[...] = oh.astype(bf16)
    exchange(n, me, oh_send, oh_recv, s1, r1, True, False)
    halos = []
    for i, (src, dst, rows) in enumerate(((ice, iceh, 6), (sens, sensh, 3), (ocean, och, 8))):
        halos.append(remote(src.at[pl.ds(ROWS_DEV - rows, rows)], dst.at[0], s3.at[2 * i], r3.at[2 * i], right))
        halos.append(remote(src.at[pl.ds(0, rows)], dst.at[1], s3.at[2 * i + 1], r3.at[2 * i + 1], left))
    w = w_c[...]
    rows = iota((ROWS_DEV, nk), 0)
    cols = iota((ROWS_DEV, nk), 1)
    pick = jnp.where((cols >= rows * K) & (cols < rows * K + K), 1.0, 0.0).astype(bf16)
    wa = dot(pick, (pa * w).astype(bf16))
    wb = dot(pick, (pb * w).astype(bf16))
    w2 = jnp.concatenate([wa, wb], axis=0).astype(bf16)
    w2_out[...] = w2
    exchange(n, me, oh_send, oh_recv, s1, r1, False, True)
    got = oh_recv[...]
    oh_out[...] = got
    f_send[...] = dot(got[:, : 2 * ROWS_DEV], forc[...]).astype(bf16)
    exchange(n, me, f_send, f_recv, s2, r2, True, False)
    for copy in halos:
        copy.start()
    exchange(n, me, f_send, f_recv, s2, r2, False, True)
    pre[...] = dot(w2, f_recv[...]).astype(bf16)
    edges = []
    for half in range(2):
        at = half * 64
        low_rows = pre.at[pl.ds(half * ROWS_DEV, 16)]
        high_rows = pre.at[pl.ds(half * ROWS_DEV + 16, 16)]
        edges.append(remote(high_rows, prex.at[pl.ds(at, 16)], s3.at[6 + 2 * half], r3.at[6 + 2 * half], right))
        edges.append(remote(low_rows, prex.at[pl.ds(at + 48, 16)], s3.at[7 + 2 * half], r3.at[7 + 2 * half], left))
        prex[pl.ds(at + 16, ROWS_DEV), :] = pre[pl.ds(half * ROWS_DEV, ROWS_DEV), :]
    for copy in edges:
        copy.start()
    for copy in halos:
        copy.wait()
    for copy in edges:
        copy.wait()
    pre_out[...] = prex[...]


def layers_kernel(
    n, ice, sens, ocean, iceh, sensh, och, pre, col_map, lift, cw, cb, w2,
    img, sg, terms,
    xa, xb, s0, s1, s2, mask, g, h3, wf, wb, oc, icr, fg, pr2,
):
    me = lax.axis_index("tile")
    keep_low = jnp.where(me == 0, 0.0, 1.0)
    keep_high = jnp.where(me == n - 1, 0.0, 1.0)
    rows = iota((128, 128), 0)
    diag = jnp.where(rows == iota((128, 128), 1), 1.0, 0.0)
    ones = jnp.ones((128, 128), bf16)
    not_first = rows > 0
    not_last = rows < 127

    def put(dst, pair, half, v):
        at = half * 384
        dst[pair, :, at : at + 128] = jnp.where(not_first, pltpu.roll(v, 1, 0), 0.0).astype(bf16)
        dst[pair, :, at + 128 : at + 256] = v.astype(bf16)
        dst[pair, :, at + 256 : at + 384] = jnp.where(not_last, pltpu.roll(v, 127, 0), 0.0).astype(bf16)

    oc[0:8, :] = och[0].astype(f32) * keep_low
    oc[8:40, :] = ocean[...].astype(f32)
    oc[40:48, :] = och[1].astype(f32) * keep_high

    def spread(e, carry):
        mask[e] = dot((diag * oc[pl.ds(e, 1), :]).astype(bf16), ones)
        return carry

    lax.fori_loop(2, 46, spread, 0)

    for i in range(6):
        put(xa, (2 + i) // 2, i % 2, iceh[0, i].astype(f32) * keep_low)
        put(xa, (40 + i) // 2, i % 2, iceh[1, i].astype(f32) * keep_high)

    def fill(q, carry):
        put(xa, q + 4, 0, ice[2 * q].astype(f32))
        put(xa, q + 4, 1, ice[2 * q + 1].astype(f32))
        return carry

    lax.fori_loop(0, ROWS_DEV // 2, fill, 0)
    zero = jnp.zeros((128, 384), bf16)
    xb[1, :, 0:384] = zero
    xb[22, :, 384:768] = zero
    for i in range(3):
        g[5 + i] = sensh[0, i].astype(f32)
        g[40 + i] = sensh[1, i].astype(f32)
    g[43] = jnp.zeros((128, 128), f32)
    g[44] = jnp.zeros((128, 128), f32)

    def fill_g(r, carry):
        g[r + 8] = sens[r].astype(f32)
        return carry

    lax.fori_loop(0, ROWS_DEV, fill_g, 0)

    icr[...] = jnp.zeros_like(icr)
    cm = col_map[...].astype(bf16)
    ext = iota((64, 128), 0)
    low_edge = jnp.where(ext < 16, keep_low, 1.0)
    edge = low_edge * jnp.where(ext >= 48, keep_high, 1.0)
    for half in range(2):
        for i in range(5):
            x = pre[half * 64 : half * 64 + 64, i * 128 : i * 128 + 128]
            icr[:, half * 5 + i, :] = dot(x, cm) * edge
    lift16 = lift[...]

    for j in range(4):
        for s in range(2):
            if not 0 <= j - s <= 2:
                wf[j * 384 : j * 384 + 384, s * 128 : s * 128 + 128] = jnp.zeros((384, 128), bf16)
                wb[s * 128 : s * 128 + 128, j * 384 : j * 384 + 384] = jnp.zeros((128, 384), bf16)

    def set_forward(layer):
        for j in range(4):
            for s in range(2):
                if 0 <= j - s <= 2:
                    for b in range(3):
                        at = j * 384 + b * 128
                        wf[at : at + 128, s * 128 : s * 128 + 128] = cw[layer * 9 + (j - s) * 3 + b]

    def set_backward(layer):
        for j in range(4):
            for s in range(2):
                if 0 <= j - s <= 2:
                    for b in range(3):
                        at = j * 384 + b * 128
                        wb[s * 128 : s * 128 + 128, at : at + 128] = cw[layer * 9 + (2 - j + s) * 3 + 2 - b]

    def run(x, q_first, pairs, count, forward, finish):
        def chunk(c, carry):
            q0 = q_first + c * pairs
            left = x[pl.ds(q0, pairs)].reshape(pairs * 128, 768)
            right = x[pl.ds(q0 + 1, pairs)].reshape(pairs * 128, 768)
            if forward:
                acc = dot(left, wf[0:768, :]) + dot(right, wf[768:1536, :])
            else:
                acc = dot(left, wb[:, 0:768], 1, 1) + dot(right, wb[:, 768:1536], 1, 1)
            for i in range(pairs):
                for s in range(2):
                    part = acc[i * 128 : i * 128 + 128, s * 128 : s * 128 + 128]
                    finish(2 * (q0 + i) + 1 + s, q0 + i + s, 1 - s, part)
            return carry

        lax.fori_loop(0, count, chunk, 0)

    def middle(x, pair, half):
        return x[pair, :, half * 384 + 128 : half * 384 + 256].astype(f32)

    def forward_step(layer, x, keep):
        bias = cb[layer : layer + 1, :]

        def step(e, pair, half, acc):
            t = jnp.tanh(acc + bias)
            m = mask[e]
            keep[e] = m * (1.0 - t * t)
            return (middle(x, pair, half) + m * t).astype(bf16)

        return step

    step0, step1, step2 = forward_step(0, xa, s0), forward_step(1, xb, s1), forward_step(2, xa, s2)

    def finish0(e, pair, half, acc):
        h = step0(e, pair, half, acc).astype(f32)
        lifted = dot(icr[e + 8].astype(bf16), lift16, 0, 0)
        put(xb, pair, half, h + lifted)

    def finish1(e, pair, half, acc):
        put(xa, pair, half, step1(e, pair, half, acc).astype(f32))

    def finish2(e, pair, half, acc):
        h3[e] = step2(e, pair, half, acc)
        put(xb, pair, half, g[e] * s2[e])

    def back2(e, pair, half, acc):
        total = g[e] + acc
        g[e] = total
        put(xa, pair, half, total * s1[e])

    def back1(e, pair, half, acc):
        total = g[e] + acc
        g[e] = total
        put(xb, pair, half, total * s0[e])

    def back0(e, pair, half, acc):
        g[e] = g[e] + acc

    set_forward(0)
    run(xa, 1, 7, 3, True, finish0)
    set_forward(1)
    run(xb, 1, 7, 3, True, finish1)
    set_forward(2)
    run(xa, 2, 5, 4, True, finish2)
    img[...] = h3[8:40]
    set_backward(2)
    run(xb, 2, 5, 4, False, back2)
    set_backward(1)
    run(xa, 3, 6, 3, False, back1)

    def project(r, carry):
        fg[r] = dot(lift16, g[r + 8].astype(bf16), 1, 1)
        return carry

    lax.fori_loop(0, ROWS_DEV, project, 0)
    fg[...] = dot(fg[...].reshape(ROWS_DEV * FP, 128).astype(bf16), cm, 1, 1).reshape(ROWS_DEV, FP, 128)
    for half in range(2):
        for i in range(5):
            pr2[half * 32 : half * 32 + 32, i * 128 : i * 128 + 128] = fg[:, half * 5 + i, :].astype(bf16)
    terms[...] = dot(w2[...], pr2[...], 0, 0).astype(bf16)

    set_backward(0)
    run(xb, 3, 6, 3, False, back0)
    sg[...] = g[8:40].astype(bf16)


def return_kernel(n, terms, oh, out, recv, ss, rs):
    me = lax.axis_index("tile")
    enter(n, me)
    exchange(n, me, terms, recv, ss, rs, True, True)
    out[...] = dot(oh[:, : 2 * ROWS_DEV], recv[...], 0, 0)


def call(kernel, outs, scratch, ins, collective=None):
    params = dict(vmem_limit_bytes=50 * 1024 * 1024)
    if collective is not None:
        params.update(collective_id=collective, has_side_effects=True)
    vmem = pl.BlockSpec(memory_space=pltpu.VMEM)
    return pl.pallas_call(
        kernel,
        out_shape=[jax.ShapeDtypeStruct(s, d) for s, d in outs],
        in_specs=[vmem] * ins,
        out_specs=[vmem] * len(outs),
        scratch_shapes=scratch,
        compiler_params=pltpu.CompilerParams(**params),
    )


def body(
    forcing, ice_state, sensitivity, owner_device, panel_slot, row_offset,
    intersection_weight, col_map, ocean_mask, lift_weight, conv_weight, conv_bias,
):
    n = lax.axis_size("tile")
    nb = n * BLK
    nk = ROWS_DEV * K
    V, D = pltpu.VMEM, pltpu.SemaphoreType.DMA
    pr = forcing.shape[1]
    own_c = owner_device.reshape(nk, 1)
    own_r = owner_device.reshape(1, nk)
    loc_c = (panel_slot * pr + row_offset).reshape(nk, 1)
    w_c = intersection_weight.reshape(nk, 1)
    forc = forcing.reshape(ROWS_DEV, 2, 5, 128).transpose(1, 0, 2, 3).reshape(2 * ROWS_DEV, HALF)
    pre, oh, w2, iceh, sensh, och = call(
        functools.partial(gather_kernel, n),
        [((128, HALF), bf16), ((nb, 128), bf16), ((64, nb), bf16),
         ((2, 6, 128, 128), bf16), ((2, 3, 128, 128), bf16), ((2, 8, 128), jnp.int32)],
        [V((nb, 128), bf16), V((nb, 128), bf16), V((nb, HALF), bf16), V((nb, HALF), bf16),
         V((64, HALF), bf16), V((128, HALF), bf16),
         D((n,)), D((n,)), D((n,)), D((n,)), D((10,)), D((10,))],
        8, 1,
    )(ice_state, sensitivity, ocean_mask, own_c, own_r, loc_c, w_c, forc)
    lift16 = jnp.pad(lift_weight, ((0, FP - F), (0, 0)))
    field = (E, 128, 128)
    img, sg, terms = call(
        functools.partial(layers_kernel, n),
        [((ROWS_DEV, 128, 128), bf16), ((ROWS_DEV, 128, 128), bf16), ((nb, HALF), bf16)],
        [V((E // 2, 128, 768), bf16), V((E // 2, 128, 768), bf16), V(field, f32), V(field, f32),
         V(field, f32), V(field, f32), V(field, f32), V(field, bf16),
         V((1536, 256), bf16), V((256, 1536), bf16), V((E, 128), f32), V((64, FP, 128), f32),
         V((ROWS_DEV, FP, 128), f32), V((64, HALF), bf16)],
        12,
    )(ice_state, sensitivity, ocean_mask, iceh, sensh, och, pre, col_map, lift16,
      conv_weight.reshape(27, 128, 128), conv_bias, w2)
    (grad,) = call(
        functools.partial(return_kernel, n),
        [((2 * ROWS_DEV, HALF), f32)],
        [V((nb, HALF), bf16), D((n,)), D((n,))],
        2, 2,
    )(terms, oh)
    grad = grad.reshape(2, ROWS_DEV, 5, 128).transpose(1, 0, 2, 3).reshape(forcing.shape)
    return img, sg, grad


def solution(mesh):
    in_specs = (
        P(("member", "tile"), None, None, None),
        P(("member", "tile"), None, None),
        P(("member", "tile"), None, None),
        P("tile", None),
        P("tile", None),
        P("tile", None),
        P("tile", None),
        P(),
        P("tile", None),
        P(),
        P(),
        P(),
    )
    out_specs = (
        P(("member", "tile"), None, None),
        P(("member", "tile"), None, None),
        P(("member", "tile"), None, None, None),
    )
    return jax.shard_map(body, mesh=mesh, in_specs=in_specs, out_specs=out_specs, check_vma=False)
```

profile of v0, /device:TPU:13, one launch (start us, length us, event | category | flops | bytes accessed | tf_op | source)
XLA Modules:
  0.0 99.2 jit_solution(12738981620682304478)
XLA Ops:
  0.6 0.0 copy-start.7
  0.6 0.7 multiply_add_fusion
  1.3 0.0 copy-done.7
  1.4 0.0 copy-start.8
  1.4 0.1 copy.24
  1.5 0.6 copy-done.8
  2.0 0.1 copy.22
  2.1 0.0 copy-start.9
  2.1 0.1 reshape.34.own_r
  2.2 0.6 copy-done.9
  2.8 0.1 copy.25
  2.9 0.1 reshape.44.w_c
  3.0 0.0 copy-start.6
  3.0 0.1 reshape.42.own_c
  3.1 0.1 reshape.43.loc_c
  3.1 0.7 copy-done.6
  3.9 0.0 copy-start.4
  4.0 0.7 copy-done.4
  4.7 0.0 copy-start
  4.7 1.2 %copy-done = bf16[32,128,128]{2,1,0:T(8,128)(2,1)S(1)} copy-done((bf16[32,128,128]{2,1,0:T(8,128)(2,1)S(1)}, bf16[32,128,128]{2,1,0:T(8,128)(2,1)}, u32[]{:S(2)}) %copy-start) | copy-done | bytes 1048600
  5.9 0.0 copy-start.1
  5.9 1.2 %copy-done.1 = bf16[32,128,128]{2,1,0:T(8,128)(2,1)S(1)} copy-done((bf16[32,128,128]{2,1,0:T(8,128)(2,1)S(1)}, bf16[32,128,128]{2,1,0:T(8,128)(2,1)}, u32[]{:S(2)}) %copy-start.1) | copy-done | bytes 1048600
  7.1 0.0 copy-start.2
  7.1 0.0 copy-start.3
  7.1 34.2 %shard_map.139 = (bf16[128,640]{1,0:T(8,128)(2,1)S(1)}, bf16[512,128]{1,0:T(8,128)(2,1)S(1)}, bf16[64,512]{1,0:T(8,128)(2,1)S(1)}, bf16[2,6,128,128]{3,2,1,0:T(8...) custom-call(bf16[32,128,128]{2,1,0:T(8,128)(2,1)S(1)} %copy-done, ...), custom_call_target="tpu_custom_call" | custom-call | tf_op jit(solution)/shard_map/pallas_call | solution.py:346
  41.4 0.0 copy-start.5
  41.4 0.0 copy-done.2
  41.4 0.0 copy-done.3
  41.4 0.7 copy-done.5
  42.0 35.1 %shard_map.140 = (bf16[32,128,128]{2,1,0:T(8,128)(2,1)}, bf16[32,128,128]{2,1,0:T(8,128)(2,1)}, bf16[512,640]{1,0:T(8,128)(2,1)S(1)}) custom-call(bf16[32,128,128]{2,1,0:T(8,128)(2,1)S(1)} %copy-done, bf16[32,128,128]{2,1,0:T(8,128)(2,1)} %sens.3, s32[32,128]{1,0:T(8,128)S(1)} %copy-done.4, bf16[2,6,128,128]{3,2,1,0:T(8,128)(2,1)S(1)} %get-tuple-element.12.iceh, ...), custom_call_target="tpu_custom_call" | custom-call | tf_op jit(solution)/shard_map/pallas_call | solution.py:357
  77.1 21.3 %shard_map.141 = f32[64,640]{1,0:T(8,128)S(1)} custom-call(bf16[512,640]{1,0:T(8,128)(2,1)S(1)} %get-tuple-element.19.terms, bf16[512,128]{1,0:T(8,128)(2,1)S(1)} %get-tuple-element.20.oh), custom_call_target="tpu_custom_call" | custom-call | tf_op jit(solution)/shard_map/pallas_call | solution.py:367
  98.5 0.7 copy.32
  (6 shorter events, 0.1 us)
Async XLA Ops:
  0.6 0.7 copy-start.7
  1.4 0.7 copy-start.8
  2.1 0.7 copy-start.9
  3.0 0.9 copy-start.6
  3.9 0.7 copy-start.4
  4.7 1.2 %copy-start = (bf16[32,128,128]{2,1,0:T(8,128)(2,1)S(1)}, bf16[32,128,128]{2,1,0:T(8,128)(2,1)}, u32[]{:S(2)}) copy-start(bf16[32,128,128]{2,1,0:T(8,128)(2,1)} %ice.3) | copy-start | bytes 3145732
  5.9 1.2 %copy-start.1 = (bf16[32,128,128]{2,1,0:T(8,128)(2,1)S(1)}, bf16[32,128,128]{2,1,0:T(8,128)(2,1)}, u32[]{:S(2)}) copy-start(bf16[32,128,128]{2,1,0:T(8,128)(2,1)} %sens.3) | copy-start | bytes 3145732
  7.1 34.3 %copy-start.2 = (bf16[3,3,3,128,128]{4,3,2,1,0:T(8,128)(2,1)S(1)}, bf16[3,3,3,128,128]{4,3,2,1,0:T(8,128)(2,1)}, u32[]{:S(2)}) copy-start(bf16[3,3,3,128,128]{4,3,2,1,0:T(8,128)(2,1)} %param.22) | copy-start | bytes 2654212
  7.1 34.3 %copy-start.3 = (f32[128,128]{1,0:T(8,128)S(1)}, f32[128,128]{1,0:T(8,128)}, u32[]{:S(2)}) copy-start(f32[128,128]{1,0:T(8,128)} %col_map.1) | copy-start | bytes 196612
  41.4 0.7 copy-start.5
where the time goes:
time: 99.6 us; the launch traced here: 99.2 us
  Pallas kernels  90.6 us (91%)
  local copies, waits for them, and re-layouts  7.12 us (7%)
    pallas_call x1, Pallas kernels, body(): call(functools.partial(layers_kernel, n), [((ROWS_DEV, 128, 128), bf16),...  35.1 us
    pallas_call x1, Pallas kernels, body(): call(functools.partial(gather_kernel, n), [((128, HALF), bf16), ((nb, 128...  34.2 us
    pallas_call x1, Pallas kernels, body(): call(functools.partial(return_kernel, n), [((2 * ROWS_DEV, HALF), f32)],...  21.3 us
    unnamed x25, local copies, waits for them, and re-layouts  6.59 us

commit v1 on v0

v1 whole, which is shorter than its diff:
```python
import functools

import jax
import jax.numpy as jnp
from jax import lax
from jax.experimental import pallas as pl
from jax.experimental.pallas import tpu as pltpu
from jax.sharding import PartitionSpec as P

F = 10
K = 4
ROWS_DEV = 32
FP = 16
HALF = 640
BLK = 16
E = 48
TRANSPOSED = False
f32, bf16 = jnp.float32, jnp.bfloat16


def dot(a, b, ca=1, cb=0):
    return lax.dot_general(a, b, (((ca,), (cb,)), ((), ())), preferred_element_type=f32)


def iota(shape, dim):
    return lax.broadcasted_iota(jnp.int32, shape, dim)


def remote(src, dst, send, recv, target):
    return pltpu.make_async_remote_copy(
        src_ref=src, dst_ref=dst, send_sem=send, recv_sem=recv,
        device_id={"tile": target}, device_id_type=pl.DeviceIdType.MESH,
    )


def block(ref, p):
    return ref.at[pl.ds(pl.multiple_of(p * BLK, BLK), BLK)]


def exchange(n, me, src, dst, send, recv, start, wait):
    def begin(step, carry):
        to = lax.rem(me + step, n)
        remote(block(src, to), block(dst, me), send.at[step], recv.at[step], to).start()
        return carry

    def finish(step, carry):
        to = lax.rem(me + step, n)
        source = lax.rem(me + n - step, n)
        remote(block(src, to), block(dst, source), send.at[step], recv.at[step], to).wait()
        return carry

    if start:
        lax.fori_loop(1, n, begin, 0)
        mine = pl.ds(pl.multiple_of(me * BLK, BLK), BLK)
        dst[mine, :] = src[mine, :]
    if wait:
        lax.fori_loop(1, n, finish, 0)


def program_kernel(
    n, transposed, ice, sens, ocean, own_t, slot_t, off_t, w_t, forc, col_map, lift, cw, cb,
    img, sg, grad,
    oh_send, oh_recv, f_send, f_recv, t_send, t_recv, f2, pre, prex, iceh, sensh, och,
    xa, xb, s0, s1, s2, mask, g, h3, wf, wb, oc, icr, fg, pr2, icev, sensv, cwv,
    ss1, rs1, ss2, rs2, ss3, rs3, ss4, rs4, ls,
):
    me = lax.axis_index("tile")
    right, left = lax.rem(me + 1, n), lax.rem(me + n - 1, n)
    nb = n * BLK
    nk = ROWS_DEV * K
    load_ice = pltpu.make_async_copy(ice, icev, ls.at[0])
    load_sens = pltpu.make_async_copy(sens, sensv, ls.at[1])
    load_cw = pltpu.make_async_copy(cw, cwv, ls.at[2])
    load_ice.start()
    load_cw.start()
    load_sens.start()
    barrier = pltpu.get_barrier_semaphore()

    def greet(step, carry):
        pl.semaphore_signal(
            barrier, inc=1, device_id={"tile": lax.rem(me + step, n)},
            device_id_type=pl.DeviceIdType.MESH,
        )
        return carry

    lax.fori_loop(1, n, greet, 0)

    eye32 = iota((ROWS_DEV, ROWS_DEV), 0) == iota((ROWS_DEV, ROWS_DEV), 1)

    def column(x):
        return jnp.concatenate(
            [jnp.sum(jnp.where(eye32, x[k : k + 1, :], 0.0), axis=1, keepdims=True) for k in range(K)], axis=0
        )

    own = column(own_t[...].astype(f32))
    loc = column((slot_t[...] * forc.shape[2] + off_t[...]).astype(f32))
    w = column(w_t[...])
    eye = iota((nk, nk), 0) == iota((nk, nk), 1)
    own_row = jnp.sum(jnp.where(eye, own, 0.0), axis=0, keepdims=True)
    earlier = iota((nk, nk), 1) < iota((nk, nk), 0)
    rank = jnp.sum(jnp.where((own == own_row) & earlier, 1.0, 0.0), axis=1, keepdims=True)
    col = (own * BLK + rank).astype(jnp.int32)
    loc = loc.astype(jnp.int32)
    lane = iota((nk, nb), 1)
    pa = jnp.where(col == lane, 1.0, 0.0)
    pb = jnp.where(col + 8 == lane, 1.0, 0.0)
    low = iota((nk, 128), 1)
    la = jnp.where(loc == low, 1.0, 0.0)
    lb = jnp.where(loc + ROWS_DEV == low, 1.0, 0.0)
    oh = dot(pa.astype(bf16), la.astype(bf16), 0, 0) + dot(pb.astype(bf16), lb.astype(bf16), 0, 0)
    oh_send[...] = oh.astype(bf16)
    pl.semaphore_wait(barrier, n - 1)
    exchange(n, me, oh_send, oh_recv, ss1, rs1, True, False)
    halos = []
    for i, (src, dst, rows) in enumerate(((ice, iceh, 6), (ocean, och, 8), (sens, sensh, 3))):
        halos.append(remote(src.at[pl.ds(ROWS_DEV - rows, rows)], dst.at[0], ss3.at[2 * i], rs3.at[2 * i], right))
        halos.append(remote(src.at[pl.ds(0, rows)], dst.at[1], ss3.at[2 * i + 1], rs3.at[2 * i + 1], left))
    for copy in halos:
        copy.start()
    rows = iota((ROWS_DEV, nk), 0)
    pick = jnp.where(lax.rem(iota((ROWS_DEV, nk), 1), ROWS_DEV) == rows, 1.0, 0.0).astype(bf16)
    w2 = jnp.concatenate([dot(pick, (pa * w).astype(bf16)), dot(pick, (pb * w).astype(bf16))], axis=0).astype(bf16)
    for q in range(forc.shape[0]):
        for half in range(2):
            for i in range(5):
                f2[half * 32 + q * 8 : half * 32 + q * 8 + 8, i * 128 : i * 128 + 128] = (
                    forc[q, half * 5 + i].astype(f32)
                )
    exchange(n, me, oh_send, oh_recv, ss1, rs1, False, True)
    f_send[...] = dot(oh_recv[:, : 2 * ROWS_DEV], f2[...].astype(bf16)).astype(bf16)
    exchange(n, me, f_send, f_recv, ss2, rs2, True, False)

    keep_low = jnp.where(me == 0, 0.0, 1.0)
    keep_high = jnp.where(me == n - 1, 0.0, 1.0)
    rows = iota((128, 128), 0)
    diag = jnp.where(rows == iota((128, 128), 1), 1.0, 0.0)
    ones = jnp.ones((128, 128), bf16)
    not_first = rows > 0
    not_last = rows < 127

    def put(dst, pair, half, v):
        at = half * 384
        dst[pair, :, at : at + 128] = jnp.where(not_first, pltpu.roll(v, 1, 0), 0.0).astype(bf16)
        dst[pair, :, at + 128 : at + 256] = v.astype(bf16)
        dst[pair, :, at + 256 : at + 384] = jnp.where(not_last, pltpu.roll(v, 127, 0), 0.0).astype(bf16)

    for copy in halos:
        copy.wait()
    load_ice.wait()
    load_sens.wait()
    load_cw.wait()
    oc[0:8, :] = och[0].astype(f32) * keep_low
    oc[8:40, :] = ocean[...].astype(f32)
    oc[40:48, :] = och[1].astype(f32) * keep_high

    def spread(e, carry):
        mask[e] = dot((diag * oc[pl.ds(e, 1), :]).astype(bf16), ones)
        return carry

    lax.fori_loop(2, 46, spread, 0)

    for i in range(6):
        put(xa, (2 + i) // 2, i % 2, iceh[0, i].astype(f32) * keep_low)
        put(xa, (40 + i) // 2, i % 2, iceh[1, i].astype(f32) * keep_high)

    def fill(q, carry):
        put(xa, q + 4, 0, icev[2 * q].astype(f32))
        put(xa, q + 4, 1, icev[2 * q + 1].astype(f32))
        return carry

    lax.fori_loop(0, ROWS_DEV // 2, fill, 0)
    zero = jnp.zeros((128, 384), bf16)
    xb[1, :, 0:384] = zero
    xb[22, :, 384:768] = zero
    for i in range(3):
        g[5 + i] = sensh[0, i].astype(f32)
        g[40 + i] = sensh[1, i].astype(f32)
    g[43] = jnp.zeros((128, 128), f32)
    g[44] = jnp.zeros((128, 128), f32)

    def fill_g(r, carry):
        g[r + 8] = sensv[r].astype(f32)
        return carry

    lax.fori_loop(0, ROWS_DEV, fill_g, 0)

    for j in range(4):
        for s in range(2):
            if not 0 <= j - s <= 2:
                wf[j * 384 : j * 384 + 384, s * 128 : s * 128 + 128] = jnp.zeros((384, 128), bf16)
                if not transposed:
                    wb[s * 128 : s * 128 + 128, j * 384 : j * 384 + 384] = jnp.zeros((128, 384), bf16)

    def set_forward(layer):
        for j in range(4):
            for s in range(2):
                if 0 <= j - s <= 2:
                    for b in range(3):
                        at = j * 384 + b * 128
                        wf[at : at + 128, s * 128 : s * 128 + 128] = cwv[layer * 9 + (j - s) * 3 + b]

    def set_backward_transposed(layer):
        for a in range(3):
            for b in range(3):
                tile = cwv[layer * 9 + (2 - a) * 3 + 2 - b].T
                for s in range(2):
                    at = (a + s) * 384 + b * 128
                    wf[at : at + 128, s * 128 : s * 128 + 128] = tile

    def set_backward(layer):
        if transposed:
            return set_backward_transposed(layer)
        for j in range(4):
            for s in range(2):
                if 0 <= j - s <= 2:
                    for b in range(3):
                        at = j * 384 + b * 128
                        wb[s * 128 : s * 128 + 128, at : at + 128] = cwv[layer * 9 + (2 - j + s) * 3 + 2 - b]

    def run(x, q_first, pairs, count, forward, finish):
        def chunk(c, carry):
            q0 = q_first + c * pairs
            left = x[pl.ds(q0, pairs)].reshape(pairs * 128, 768)
            right = x[pl.ds(q0 + 1, pairs)].reshape(pairs * 128, 768)
            if forward or transposed:
                acc = dot(left, wf[0:768, :]) + dot(right, wf[768:1536, :])
            else:
                acc = dot(left, wb[:, 0:768], 1, 1) + dot(right, wb[:, 768:1536], 1, 1)
            for i in range(pairs):
                for s in range(2):
                    part = acc[i * 128 : i * 128 + 128, s * 128 : s * 128 + 128]
                    finish(2 * (q0 + i) + 1 + s, q0 + i + s, 1 - s, part)
            return carry

        lax.fori_loop(0, count, chunk, 0)

    def middle(x, pair, half):
        return x[pair, :, half * 384 + 128 : half * 384 + 256].astype(f32)

    def forward_step(layer, x, keep):
        bias = cb[layer : layer + 1, :]

        def step(e, pair, half, acc):
            t = jnp.tanh(acc + bias)
            m = mask[e]
            keep[e] = m * (1.0 - t * t)
            return (middle(x, pair, half) + m * t).astype(bf16)

        return step

    step0, step1, step2 = forward_step(0, xa, s0), forward_step(1, xb, s1), forward_step(2, xa, s2)

    def finish0(e, pair, half, acc):
        h3[e] = step0(e, pair, half, acc)

    set_forward(0)
    run(xa, 1, 7, 3, True, finish0)

    exchange(n, me, f_send, f_recv, ss2, rs2, False, True)
    pre[...] = dot(w2, f_recv[...]).astype(bf16)
    edges = []
    for half in range(2):
        at = half * 64
        low_rows = pre.at[pl.ds(half * ROWS_DEV, 16)]
        high_rows = pre.at[pl.ds(half * ROWS_DEV + 16, 16)]
        edges.append(remote(high_rows, prex.at[pl.ds(half * 32, 16)], ss3.at[6 + 2 * half], rs3.at[6 + 2 * half], right))
        edges.append(remote(low_rows, prex.at[pl.ds(half * 32 + 16, 16)], ss3.at[7 + 2 * half], rs3.at[7 + 2 * half], left))
    for copy in edges:
        copy.start()
    icr[...] = jnp.zeros_like(icr)
    cm = col_map[...].astype(bf16)
    for half in range(2):
        for i in range(5):
            x = pre[half * 32 : half * 32 + 32, i * 128 : i * 128 + 128]
            icr[16:48, half * 5 + i, :] = dot(x, cm)
    lift16 = lift[...]

    def lifted(e):
        return h3[e].astype(f32) + dot(icr[e + 8].astype(bf16), lift16, 0, 0)

    def lift_pair(q, carry):
        put(xb, q, 0, lifted(2 * q))
        put(xb, q, 1, lifted(2 * q + 1))
        return carry

    set_forward(1)
    lax.fori_loop(4, 20, lift_pair, 0)
    for copy in edges:
        copy.wait()
    for half in range(2):
        for i in range(5):
            x = prex[half * 32 : half * 32 + 32, i * 128 : i * 128 + 128]
            y = dot(x, cm)
            icr[0:16, half * 5 + i, :] = y[0:16] * keep_low
            icr[48:64, half * 5 + i, :] = y[16:32] * keep_high
    for e in (3, 4, 5, 6, 7, 40, 41, 42, 43, 44):
        put(xb, e // 2, e % 2, lifted(e))

    def finish1(e, pair, half, acc):
        put(xa, pair, half, step1(e, pair, half, acc).astype(f32))

    def finish2(e, pair, half, acc):
        h3[e] = step2(e, pair, half, acc)
        put(xb, pair, half, g[e] * s2[e])

    def back2(e, pair, half, acc):
        total = g[e] + acc
        g[e] = total
        put(xa, pair, half, total * s1[e])

    def back1(e, pair, half, acc):
        total = g[e] + acc
        g[e] = total
        put(xb, pair, half, total * s0[e])

    def back0(e, pair, half, acc):
        g[e] = g[e] + acc

    run(xb, 1, 7, 3, True, finish1)
    set_forward(2)
    run(xa, 2, 5, 4, True, finish2)
    out_img = pltpu.make_async_copy(h3.at[pl.ds(8, ROWS_DEV)], img, ls.at[3])
    out_img.start()
    set_backward(2)
    run(xb, 2, 5, 4, False, back2)
    set_backward(1)
    run(xa, 3, 6, 3, False, back1)

    def project(r, carry):
        fg[r] = dot(lift16, g[r + 8].astype(bf16), 1, 1)
        return carry

    lax.fori_loop(0, ROWS_DEV, project, 0)
    fg[...] = dot(fg[...].reshape(ROWS_DEV * FP, 128).astype(bf16), cm, 1, 1).reshape(ROWS_DEV, FP, 128)
    for half in range(2):
        for i in range(5):
            pr2[half * 32 : half * 32 + 32, i * 128 : i * 128 + 128] = fg[:, half * 5 + i, :].astype(bf16)
    t_send[...] = dot(w2, pr2[...], 0, 0).astype(bf16)
    exchange(n, me, t_send, t_recv, ss4, rs4, True, False)
    set_backward(0)
    run(xb, 3, 6, 3, False, back0)
    icev[...] = g[8:40].astype(bf16)
    out_sg = pltpu.make_async_copy(icev, sg, ls.at[4])
    out_sg.start()
    exchange(n, me, t_send, t_recv, ss4, rs4, False, True)
    total = dot(oh_recv[:, : 2 * ROWS_DEV], t_recv[...], 0, 0)
    for q in range(grad.shape[0]):
        for half in range(2):
            for i in range(5):
                grad[q, half * 5 + i] = total[half * 32 + q * 8 : half * 32 + q * 8 + 8, i * 128 : i * 128 + 128]
    out_img.wait()
    out_sg.wait()


def body(
    forcing, ice_state, sensitivity, owner_device, panel_slot, row_offset,
    intersection_weight, col_map, ocean_mask, lift_weight, conv_weight, conv_bias,
):
    n = lax.axis_size("tile")
    nb = n * BLK
    V, D = pltpu.VMEM, pltpu.SemaphoreType.DMA
    vmem, hbm = pl.BlockSpec(memory_space=pltpu.VMEM), pl.BlockSpec(memory_space=pl.ANY)
    panels, pr = forcing.shape[:2]
    lift16 = jnp.pad(lift_weight, ((0, FP - F), (0, 0)))
    field = (E, 128, 128)
    tile = (ROWS_DEV, 128, 128)
    img, sg, grad = pl.pallas_call(
        functools.partial(program_kernel, n, TRANSPOSED),
        out_shape=[
            jax.ShapeDtypeStruct(tile, bf16),
            jax.ShapeDtypeStruct(tile, bf16),
            jax.ShapeDtypeStruct((panels, F, pr, 128), f32),
        ],
        in_specs=[hbm, hbm] + [vmem] * 8 + [hbm, vmem],
        out_specs=[hbm, hbm, vmem],
        scratch_shapes=[
            V((nb, 128), bf16), V((nb, 128), bf16), V((nb, HALF), bf16), V((nb, HALF), bf16),
            V((nb, HALF), bf16), V((nb, HALF), bf16), V((64, HALF), f32), V((64, HALF), bf16), V((64, HALF), bf16),
            V((2, 6, 128, 128), bf16), V((2, 3, 128, 128), bf16), V((2, 8, 128), jnp.int32),
            V((E // 2, 128, 768), bf16), V((E // 2, 128, 768), bf16), V(field, f32), V(field, f32),
            V(field, f32), V(field, f32), V(field, f32), V(field, bf16),
            V((1536, 256), bf16), V((256, 1536), bf16), V((E, 128), f32), V((64, FP, 128), f32),
            V((ROWS_DEV, FP, 128), f32), V((64, HALF), bf16), V(tile, bf16), V(tile, bf16), V((27, 128, 128), bf16),
            D((n,)), D((n,)), D((n,)), D((n,)), D((10,)), D((10,)), D((n,)), D((n,)), D((5,)),
        ],
        compiler_params=pltpu.CompilerParams(
            vmem_limit_bytes=56 * 1024 * 1024, collective_id=1, has_side_effects=True
        ),
    )(ice_state, sensitivity, ocean_mask, owner_device.T, panel_slot.T, row_offset.T, intersection_weight.T,
      forcing.transpose(0, 2, 1, 3), col_map, lift16, conv_weight.reshape(27, 128, 128), conv_bias)
    return img, sg, grad.transpose(0, 2, 1, 3)


def solution(mesh):
    in_specs = (
        P(("member", "tile"), None, None, None),
        P(("member", "tile"), None, None),
        P(("member", "tile"), None, None),
        P("tile", None),
        P("tile", None),
        P("tile", None),
        P("tile", None),
        P(),
        P("tile", None),
        P(),
        P(),
        P(),
    )
    out_specs = (
        P(("member", "tile"), None, None),
        P(("member", "tile"), None, None),
        P(("member", "tile"), None, None, None),
    )
    return jax.shard_map(body, mesh=mesh, in_specs=in_specs, out_specs=out_specs, check_vma=False)
```

time: 99.6 us -> 75.7 us (0.76)
  Pallas kernels: 90.6 us -> 69 us
  local copies, waits for them, and re-layouts: 7.12 us -> 5.4 us
    pallas_call x3 -> x1, Pallas kernels: 90.6 us -> 69 us  [body(): pl.pallas_call(functools.partial(program_kernel, n, TRANSPOSED), out_shap...]
    unnamed x25 -> x9, local copies, waits for them, and re-layouts: 6.59 us -> 4.8 us
where the time goes in v1:
time: 75.7 us; the launch traced here: 75 us
  Pallas kernels  69 us (91%)
  local copies, waits for them, and re-layouts  5.4 us (7%)
    pallas_call x1, Pallas kernels, body(): pl.pallas_call(functools.partial(program_kernel, n, TRANSPOSED), out_shap...  69 us
    unnamed x9, local copies, waits for them, and re-layouts  4.8 us

profile of v1, /device:TPU:13, one launch (start us, length us, event | category | flops | bytes accessed | tf_op | source)
XLA Modules:
  0.0 75.0 jit_solution(13548371394840385933)
XLA Ops:
  0.6 0.0 copy-start.2
  0.6 0.7 copy-done.2
  1.3 0.6 pad.4.lift
  1.9 69.0 %shard_map.139 = (bf16[32,128,128]{2,1,0:T(8,128)(2,1)}, bf16[32,128,128]{2,1,0:T(8,128)(2,1)}, f32[4,10,8,128]{3,2,1,0:T(8,128)}) custom-call(bf16[32,128,128]{2,1,0:T(8,128)(2,1)} %ice.1, bf16[32,128,128]{2,1,0:T(8,128)(2,1)} %sens.1, s32[32,128]{1,0:T(8,128)} %ocean.1, s32[4,32]{1,0:T(4,128)} %bitcast.10, s32[4,32]{1,0:T(4,128)} %bitcast.11, ...), custom_call_target="tpu_custom_call" | custom-call | tf_op jit(solution)/shard_map/pallas_call | solution.py:367
  70.9 0.0 copy-start
  70.9 2.4 %copy.18 = bf16[32,128,128]{2,1,0:T(8,128)(2,1)} copy(bf16[32,128,128]{2,1,0:T(8,128)(2,1)} %get-tuple-element.12) | data formatting | bytes 2097152
  73.3 0.0 copy-done
  73.3 0.0 copy-start.1
  73.3 1.0 %copy.19 = bf16[32,128,128]{2,1,0:T(8,128)(2,1)} copy(bf16[32,128,128]{2,1,0:T(8,128)(2,1)S(1)} %copy-done) | data formatting | bytes 2097152
  74.3 0.1 copy-done.1
  74.4 0.7 copy.20
Async XLA Ops:
  0.6 0.7 copy-start.2
  70.9 2.4 %copy-start = (bf16[32,128,128]{2,1,0:T(8,128)(2,1)S(1)}, bf16[32,128,128]{2,1,0:T(8,128)(2,1)}, u32[]{:S(2)}) copy-start(bf16[32,128,128]{2,1,0:T(8,128)(2,1)} %get-tuple-element.13) | copy-start | bytes 3145732
  73.3 1.1 %copy-start.1 = (f32[4,10,8,128]{3,2,1,0:T(8,128)S(1)}, f32[4,10,8,128]{3,2,1,0:T(8,128)}, u32[]{:S(2)}) copy-start(f32[4,10,8,128]{3,2,1,0:T(8,128)} %get-tuple-element.8) | copy-start | bytes 491524

commit v2 on v1

--- a/solution.py
+++ b/solution.py
@@ -61,7 +61,7 @@
     n, transposed, ice, sens, ocean, own_t, slot_t, off_t, w_t, forc, col_map, lift, cw, cb,
     img, sg, grad,
     oh_send, oh_recv, f_send, f_recv, t_send, t_recv, f2, pre, prex, iceh, sensh, och,
-    xa, xb, s0, s1, s2, mask, g, h3, wf, wb, oc, icr, fg, pr2, icev, sensv, cwv,
+    xa, xb, s0, s1, s2, mask, g, h3, wf, wb, oc, icr, fg, pr2, icev, sensv, cwv, bd,
     ss1, rs1, ss2, rs2, ss3, rs3, ss4, rs4, ls,
 ):
     me = lax.axis_index("tile")
@@ -153,11 +153,14 @@
     oc[8:40, :] = ocean[...].astype(f32)
     oc[40:48, :] = och[1].astype(f32) * keep_high
 
-    def spread(e, carry):
-        mask[e] = dot((diag * oc[pl.ds(e, 1), :]).astype(bf16), ones)
-        return carry
-
-    lax.fori_loop(2, 46, spread, 0)
+    def spread(c, carry):
+        e = 8 * c
+        cells = oc[pl.ds(pl.multiple_of(e, 8), 8), :]
+        wide = jnp.concatenate([(diag * cells[i : i + 1, :]).astype(bf16) for i in range(8)], axis=0)
+        mask[pl.ds(e, 8)] = dot(wide, ones).reshape(8, 128, 128)
+        return carry
+
+    lax.fori_loop(0, E // 8, spread, 0)
 
     for i in range(6):
         put(xa, (2 + i) // 2, i % 2, iceh[0, i].astype(f32) * keep_low)
@@ -232,7 +235,7 @@
                     finish(2 * (q0 + i) + 1 + s, q0 + i + s, 1 - s, part)
             return carry
 
-        lax.fori_loop(0, count, chunk, 0)
+        lax.fori_loop(0, count, chunk, 0, unroll=True)
 
     def middle(x, pair, half):
         return x[pair, :, half * 384 + 128 : half * 384 + 256].astype(f32)
@@ -275,16 +278,23 @@
             icr[16:48, half * 5 + i, :] = dot(x, cm)
     lift16 = lift[...]
 
-    def lifted(e):
-        return h3[e].astype(f32) + dot(icr[e + 8].astype(bf16), lift16, 0, 0)
-
-    def lift_pair(q, carry):
-        put(xb, q, 0, lifted(2 * q))
-        put(xb, q, 1, lifted(2 * q + 1))
+    eight = jnp.concatenate([lift16] * 8, axis=0)
+    of_row = iota((128, 128), 0) // FP
+    for i in range(8):
+        bd[:, i * 128 : i * 128 + 128] = jnp.where(of_row == i, eight, jnp.zeros_like(eight))
+
+    def lift_eight(c, chosen):
+        wide = dot(icr[pl.ds(8 * c + 8, 8)].reshape(8 * FP, 128).astype(bf16), bd[...], 0, 0)
+        for i in chosen:
+            v = h3[8 * c + i].astype(f32) + wide[:, i * 128 : i * 128 + 128]
+            put(xb, 4 * c + i // 2, i % 2, v)
+
+    def lift_inner(c, carry):
+        lift_eight(c, range(8))
         return carry
 
     set_forward(1)
-    lax.fori_loop(4, 20, lift_pair, 0)
+    lax.fori_loop(1, 5, lift_inner, 0)
     for copy in edges:
         copy.wait()
     for half in range(2):
@@ -293,8 +303,8 @@
             y = dot(x, cm)
             icr[0:16, half * 5 + i, :] = y[0:16] * keep_low
             icr[48:64, half * 5 + i, :] = y[16:32] * keep_high
-    for e in (3, 4, 5, 6, 7, 40, 41, 42, 43, 44):
-        put(xb, e // 2, e % 2, lifted(e))
+    lift_eight(0, range(3, 8))
+    lift_eight(5, range(5))
 
     def finish1(e, pair, half, acc):
         put(xa, pair, half, step1(e, pair, half, acc).astype(f32))
@@ -319,18 +329,18 @@
     run(xb, 1, 7, 3, True, finish1)
     set_forward(2)
     run(xa, 2, 5, 4, True, finish2)
-    out_img = pltpu.make_async_copy(h3.at[pl.ds(8, ROWS_DEV)], img, ls.at[3])
-    out_img.start()
+    img[...] = h3[8:40]
     set_backward(2)
     run(xb, 2, 5, 4, False, back2)
     set_backward(1)
     run(xa, 3, 6, 3, False, back1)
 
-    def project(r, carry):
-        fg[r] = dot(lift16, g[r + 8].astype(bf16), 1, 1)
-        return carry
-
-    lax.fori_loop(0, ROWS_DEV, project, 0)
+    def project(c, carry):
+        wide = jnp.concatenate([g[8 * c + 8 + i].astype(bf16) for i in range(8)], axis=1)
+        fg[pl.ds(8 * c, 8)] = dot(bd[...], wide, 1, 1).reshape(8, FP, 128)
+        return carry
+
+    lax.fori_loop(0, ROWS_DEV // 8, project, 0)
     fg[...] = dot(fg[...].reshape(ROWS_DEV * FP, 128).astype(bf16), cm, 1, 1).reshape(ROWS_DEV, FP, 128)
     for half in range(2):
         for i in range(5):
@@ -339,17 +349,13 @@
     exchange(n, me, t_send, t_recv, ss4, rs4, True, False)
     set_backward(0)
     run(xb, 3, 6, 3, False, back0)
-    icev[...] = g[8:40].astype(bf16)
-    out_sg = pltpu.make_async_copy(icev, sg, ls.at[4])
-    out_sg.start()
+    sg[...] = g[8:40].astype(bf16)
     exchange(n, me, t_send, t_recv, ss4, rs4, False, True)
     total = dot(oh_recv[:, : 2 * ROWS_DEV], t_recv[...], 0, 0)
     for q in range(grad.shape[0]):
         for half in range(2):
             for i in range(5):
                 grad[q, half * 5 + i] = total[half * 32 + q * 8 : half * 32 + q * 8 + 8, i * 128 : i * 128 + 128]
-    out_img.wait()
-    out_sg.wait()
 
 
 def body(
@@ -372,7 +378,7 @@
             jax.ShapeDtypeStruct((panels, F, pr, 128), f32),
         ],
         in_specs=[hbm, hbm] + [vmem] * 8 + [hbm, vmem],
-        out_specs=[hbm, hbm, vmem],
+        out_specs=[vmem, vmem, vmem],
         scratch_shapes=[
             V((nb, 128), bf16), V((nb, 128), bf16), V((nb, HALF), bf16), V((nb, HALF), bf16),
             V((nb, HALF), bf16), V((nb, HALF), bf16), V((64, HALF), f32), V((64, HALF), bf16), V((64, HALF), bf16),
@@ -380,8 +386,8 @@
             V((E // 2, 128, 768), bf16), V((E // 2, 128, 768), bf16), V(field, f32), V(field, f32),
             V(field, f32), V(field, f32), V(field, f32), V(field, bf16),
             V((1536, 256), bf16), V((256, 1536), bf16), V((E, 128), f32), V((64, FP, 128), f32),
-            V((ROWS_DEV, FP, 128), f32), V((64, HALF), bf16), V(tile, bf16), V(tile, bf16), V((27, 128, 128), bf16),
-            D((n,)), D((n,)), D((n,)), D((n,)), D((10,)), D((10,)), D((n,)), D((n,)), D((5,)),
+            V((ROWS_DEV, FP, 128), f32), V((64, HALF), bf16), V(tile, bf16), V(tile, bf16), V((27, 128, 128), bf16), V((128, 1024), bf16),
+            D((n,)), D((n,)), D((n,)), D((n,)), D((10,)), D((10,)), D((n,)), D((n,)), D((3,)),
         ],
         compiler_params=pltpu.CompilerParams(
             vmem_limit_bytes=56 * 1024 * 1024, collective_id=1, has_side_effects=True

time: 75.7 us -> 67.5 us (0.89)
  Pallas kernels: 69 us -> 61.1 us
    pallas_call x1, Pallas kernels: 69 us -> 61.1 us  [body(): pl.pallas_call(functools.partial(program_kernel, n, TRANSPOSED), out_shap...]
where the time goes in v2:
time: 67.5 us; the launch traced here: 67.1 us
  Pallas kernels  61.1 us (91%)
  local copies, waits for them, and re-layouts  5.4 us (8%)
    pallas_call x1, Pallas kernels, body(): pl.pallas_call(functools.partial(program_kernel, n, TRANSPOSED), out_shap...  61.1 us
    unnamed x9, local copies, waits for them, and re-layouts  4.8 us

profile of v2, /device:TPU:13, one launch (start us, length us, event | category | flops | bytes accessed | tf_op | source)
XLA Modules:
  0.0 67.1 jit_solution(11931149548764477202)
XLA Ops:
  0.6 0.0 copy-start.2
  0.6 0.7 %copy-done.2 = bf16[10,128]{1,0:T(8,128)(2,1)S(1)} copy-done((bf16[10,128]{1,0:T(8,128)(2,1)S(1)}, bf16[10,128]{1,0:T(8,128)(2,1)}, u32[]{:S(2)}) %copy-start.2) | copy-done | bytes 2584
  1.3 0.6 pad.4.lift
  1.9 61.1 %shard_map.139 = (bf16[32,128,128]{2,1,0:T(8,128)(2,1)}, bf16[32,128,128]{2,1,0:T(8,128)(2,1)}, f32[4,10,8,128]{3,2,1,0:T(8,128)}) custom-call(bf16[32,128,128]{2,1,0:T(8,128)(2,1)} %ice.1, bf16[32,128,128]{2,1,0:T(8,128)(2,1)} %sens.1, s32[32,128]{1,0:T(8,128)} %ocean.1, s32[4,32]{1,0:T(4,128)} %bitcast.10, s32[4,32]{1,0:T(4,128)} %bitcast.11, ...), custom_call_target="tpu_custom_call" | custom-call | tf_op jit(solution)/shard_map/pallas_call | solution.py:373
  63.0 0.0 copy-start
  63.0 2.4 %copy.18 = bf16[32,128,128]{2,1,0:T(8,128)(2,1)} copy(bf16[32,128,128]{2,1,0:T(8,128)(2,1)} %get-tuple-element.12) | data formatting | bytes 2097152
  65.4 0.0 copy-done
  65.4 0.0 copy-start.1
  65.4 1.0 %copy.19 = bf16[32,128,128]{2,1,0:T(8,128)(2,1)} copy(bf16[32,128,128]{2,1,0:T(8,128)(2,1)S(1)} %copy-done) | data formatting | bytes 2097152
  66.4 0.1 copy-done.1
  66.5 0.7 copy.20
Async XLA Ops:
  0.6 0.7 %copy-start.2 = (bf16[10,128]{1,0:T(8,128)(2,1)S(1)}, bf16[10,128]{1,0:T(8,128)(2,1)}, u32[]{:S(2)}) copy-start(bf16[10,128]{1,0:T(8,128)(2,1)} %param.21) | copy-start | bytes 7684
  63.0 2.4 %copy-start = (bf16[32,128,128]{2,1,0:T(8,128)(2,1)S(1)}, bf16[32,128,128]{2,1,0:T(8,128)(2,1)}, u32[]{:S(2)}) copy-start(bf16[32,128,128]{2,1,0:T(8,128)(2,1)} %get-tuple-element.13) | copy-start | bytes 3145732
  65.4 1.1 %copy-start.1 = (f32[4,10,8,128]{3,2,1,0:T(8,128)S(1)}, f32[4,10,8,128]{3,2,1,0:T(8,128)}, u32[]{:S(2)}) copy-start(f32[4,10,8,128]{3,2,1,0:T(8,128)} %get-tuple-element.8) | copy-start | bytes 491524
